TPU v7x, 256 devices: a whole 4x4x8 slice. The times are simulated.
256 devices in a mesh: set: 32 (over y, x, core), path: 8 (over z).
Axes of the slice: x: 4, y: 4, z: 8, core: 2. Of those that a mesh axis runs over, the one named last changes fastest.
Arguments:
- start_state: float32 [4096, 2048], P(('path', 'set')), may hold values from -6 to 6
- shocks: bfloat16 [2, 4096, 2048], P(None, ('path', 'set')), may hold values from -6 to 6
- loading: bfloat16 [2048, 2048], replicated, may hold values from -0.125 to 0.125
- decay: float32 [2048], replicated, may hold values from 0.5 to 1
- factor_lists: int32 [4096, 64], P('set'), may hold values from 0 to 2047, all different within a row
- delta: bfloat16 [4096, 64], P('set'), may hold values from -0.75 to 0.75
- gamma: bfloat16 [4096, 64, 64], P('set'), may hold values from -0.09375 to 0.09375
- currency: int32 [4096], P('set'), may hold values from 0 to 15
- owner: int32 [4096], P('set'), may hold values from 0 to 255
Outputs:
- exposure: float32 [2, 256, 4096], P(None, 'set', 'path')
- end_state: float32 [4096, 2048], P(('path', 'set'))
Inputs may be any that keep to these rules, and one draw needn't show every extreme that they name: `factor_lists`: the 64 factors of one netting set are different.
All inputs are finite; a program needn't handle non-finite values.
Results may differ from a plain program's by a relative error of at most 0.004.
Values may be sent and summed in bfloat16 or wider, within the bound.
No kernel may reach another device: no remote copies, remote signals or barrier semaphores. Data moves between devices by JAX's collectives and lax.ppermute only.
A program may use at most 64 MiB of HBM per device.

v0:
```python
import math
import jax
import jax.numpy as jnp
from jax import lax
from jax.sharding import PartitionSpec as P

NB = 16
STEPS = 2
PDEV = 16
CP_DEV = 8


def value_block(slab, lists_b, delta_b, gamma_b, cur_b):
    rows = slab.shape[0]
    count = lists_b.shape[0]
    picked = jnp.take(slab, lists_b.reshape(-1), axis=1).reshape(rows, count, lists_b.shape[1])
    curved = jnp.einsum("psk,skl->psl", picked, gamma_b, preferred_element_type=jnp.float32)
    linear = delta_b.astype(jnp.float32)[None] + 0.5 * curved
    local = jnp.sum(picked.astype(jnp.float32) * linear, axis=2)
    rates = jnp.exp(0.2 * jnp.take(slab, cur_b, axis=1).astype(jnp.float32))
    return (local * rates).T


def revalue(slab, lists, delta, gamma, cur):
    total = lists.shape[0]
    width = math.gcd(16, total)
    blocks = total // width
    depth = lists.shape[1]
    stacked = lax.map(
        lambda a: value_block(slab, a[0], a[1], a[2], a[3]),
        (
            lists.reshape(blocks, width, depth),
            delta.reshape(blocks, width, depth),
            gamma.reshape(blocks, width, depth, depth),
            cur.reshape(blocks, width),
        ),
    )
    return stacked.reshape(total, slab.shape[0])


def regress(gram, moments, total):
    size = gram.shape[0]
    chol = jnp.linalg.cholesky(gram / total + 0.001 * jnp.eye(size, dtype=jnp.float32))
    middle = lax.linalg.triangular_solve(chol, moments / total, left_side=True, lower=True)
    return lax.linalg.triangular_solve(chol, middle, left_side=True, lower=True, transpose_a=True)


def per_device(start_state, shocks, loading, decay, factor_lists, delta, gamma, currency, owner):
    high = lax.Precision.HIGHEST
    groups = lax.axis_size("set")
    member = lax.axis_index("set")
    total_paths = PDEV * groups * lax.axis_size("path")
    set_count = factor_lists.shape[0]
    onehot = (owner[None, :] == jnp.arange(CP_DEV * groups, dtype=jnp.int32)[:, None]).astype(
        jnp.float32
    )
    state = start_state
    slabs = []
    evaluated = []
    for step in range(STEPS):
        state = decay[None, :] * state + jnp.dot(
            shocks[step], loading, preferred_element_type=jnp.float32
        )
        slab = state.astype(jnp.bfloat16)
        slabs.append(slab)
        piece = lax.all_gather(slab, "set", axis=0, tiled=True)
        evaluate_values = revalue(piece, factor_lists, delta, gamma, currency)
        evaluated.append(
            jnp.concatenate([evaluate_values, piece[:, :NB].astype(jnp.float32).T], axis=0)
        )
    results = []
    for step in range(STEPS):
        values = evaluated[step][:set_count]
        factors = evaluated[step][set_count:]
        summed = lax.psum(jnp.dot(onehot, values, precision=high), "set")
        netted = lax.dynamic_slice_in_dim(summed, member * CP_DEV, CP_DEV, 0)
        ones = jnp.ones((1, values.shape[1]), jnp.float32)
        basis = jnp.concatenate([ones, factors], axis=0)
        gram, moments = lax.psum(
            (jnp.dot(basis, basis.T, precision=high), jnp.dot(basis, netted.T, precision=high)),
            "path",
        )
        coef = regress(gram, moments, total_paths)
        fitted = jnp.dot(coef.T, basis, precision=high)
        results.append(jnp.maximum(netted - 0.9 * fitted, 0.0))
    return (jnp.stack(results), state)


def solution(mesh):
    return jax.shard_map(
        per_device,
        mesh=mesh,
        in_specs=(
            P(("path", "set"), None),
            P(None, ("path", "set"), None),
            P(),
            P(),
            P("set", None),
            P("set", None),
            P("set", None, None),
            P("set"),
            P("set"),
        ),
        out_specs=(P(None, "set", "path"), P(("path", "set"), None)),
        check_vma=False,
    )
```

profile of v0, /device:TPU:6, one launch (start us, length us, event | category | flops | bytes accessed | tf_op | source)
XLA Modules:
  0.0 349.1 jit_solution(17713936069963146569)
XLA Ops:
  7.2 5.4 %fusion.65 = (bf16[16,2048]{1,0:T(8,128)(2,1)}, f32[16,2048]{1,0:T(8,128)S(1)}) fusion(bf16[2048,2048]{1,0:T(8,128)(2,1)} %param.24, bf16[2,16,2048]{2,1,0:T(8,128)(2,1)} %param.23, f32[16,2048]{1,0:T(8,128)} %param.22, f32[2048]{0:T(1024)} %param.25), kind=kOutput, calls=%fused_computation.112 | convolution fusion | flops 134316032 | bytes 8790016 | tf_op jit(solution)/shard_map/dot_general | solution.py:61
  13.1 1.9 fusion.64
  16.2 4.5 %copy.13 = bf16[128,64,64]{1,2,0:T(8,128)(2,1)} copy(bf16[128,64,64]{0,2,1:T(8,128)(2,1)S(1)} %copy-done.1) | data formatting | bytes 2097152 | tf_op args[6]
  20.7 45.6 %all-gather.5.cloned.1.call-done = bf16[512,2048]{1,0:T(8,128)(2,1)} async-done(((bf16[16,2048]{1,0:T(8,128)(2,1)}), bf16[512,2048]{1,0:T(8,128)(2,1)}) %all-gather.5.cloned.1.call-update) | async-done | bytes 2097168 | tf_op jit(solution)/shard_map/all_gather | solution.py:66
  66.3 2.9 copy.17
  69.2 52.6 %while.21 = (s32[]{:T(128)}, f32[8,16,512]{2,1,0:T(8,128)S(1)}, s32[8,16,64]{2,1,0:T(8,128)S(1)}, bf16[512,2048]{0,1:T(8,128)(2,1)S(1)}, bf16[8,16,64]{2,1,0:T(8...) while((s32[]{:T(128)}, f32[8,16,512]{2,1,0:T(8,128)S(1)}, ...), condition=%wide.region_10.16_spmd, body=%wide.region_8.15_spmd.sunk | while | flops 70291552 | bytes 6755201 | solution.py:29
  70.0 4.0 %gather_fusion.2 = bf16[1024,512]{1,0:T(8,128)(2,1)S(1)} fusion(bf16[512,2048]{0,1:T(8,128)(2,1)S(1)} %get-tuple-element.254, s32[1024]{0:T(1024)S(1)} %fusion.90), kind=kCustom, calls=%fused_computation.2.clone.clone.1 | custom fusion | bytes 2101248 | tf_op jit(solution)/shard_map/while/body/eval_jaxpr/jit(_take)/gather | solution.py:16
  76.6 4.0 %gather_fusion.2 = bf16[1024,512]{1,0:T(8,128)(2,1)S(1)} fusion(bf16[512,2048]{0,1:T(8,128)(2,1)S(1)} %get-tuple-element.254, s32[1024]{0:T(1024)S(1)} %fusion.90), kind=kCustom, calls=%fused_computation.2.clone.clone.1 | custom fusion | bytes 2101248 | tf_op jit(solution)/shard_map/while/body/eval_jaxpr/jit(_take)/gather | solution.py:16
  83.1 4.0 %gather_fusion.2 = bf16[1024,512]{1,0:T(8,128)(2,1)S(1)} fusion(bf16[512,2048]{0,1:T(8,128)(2,1)S(1)} %get-tuple-element.254, s32[1024]{0:T(1024)S(1)} %fusion.90), kind=kCustom, calls=%fused_computation.2.clone.clone.1 | custom fusion | bytes 2101248 | tf_op jit(solution)/shard_map/while/body/eval_jaxpr/jit(_take)/gather | solution.py:16
  89.7 4.0 %gather_fusion.2 = bf16[1024,512]{1,0:T(8,128)(2,1)S(1)} fusion(bf16[512,2048]{0,1:T(8,128)(2,1)S(1)} %get-tuple-element.254, s32[1024]{0:T(1024)S(1)} %fusion.90), kind=kCustom, calls=%fused_computation.2.clone.clone.1 | custom fusion | bytes 2101248 | tf_op jit(solution)/shard_map/while/body/eval_jaxpr/jit(_take)/gather | solution.py:16
  96.3 4.0 %gather_fusion.2 = bf16[1024,512]{1,0:T(8,128)(2,1)S(1)} fusion(bf16[512,2048]{0,1:T(8,128)(2,1)S(1)} %get-tuple-element.254, s32[1024]{0:T(1024)S(1)} %fusion.90), kind=kCustom, calls=%fused_computation.2.clone.clone.1 | custom fusion | bytes 2101248 | tf_op jit(solution)/shard_map/while/body/eval_jaxpr/jit(_take)/gather | solution.py:16
  102.8 4.0 %gather_fusion.2 = bf16[1024,512]{1,0:T(8,128)(2,1)S(1)} fusion(bf16[512,2048]{0,1:T(8,128)(2,1)S(1)} %get-tuple-element.254, s32[1024]{0:T(1024)S(1)} %fusion.90), kind=kCustom, calls=%fused_computation.2.clone.clone.1 | custom fusion | bytes 2101248 | tf_op jit(solution)/shard_map/while/body/eval_jaxpr/jit(_take)/gather | solution.py:16
  107.0 1.5 fusion.91
  109.4 4.0 %gather_fusion.2 = bf16[1024,512]{1,0:T(8,128)(2,1)S(1)} fusion(bf16[512,2048]{0,1:T(8,128)(2,1)S(1)} %get-tuple-element.254, s32[1024]{0:T(1024)S(1)} %fusion.90), kind=kCustom, calls=%fused_computation.2.clone.clone.1 | custom fusion | bytes 2101248 | tf_op jit(solution)/shard_map/while/body/eval_jaxpr/jit(_take)/gather | solution.py:16
  113.6 1.5 fusion.91
  116.0 4.0 %gather_fusion.2 = bf16[1024,512]{1,0:T(8,128)(2,1)S(1)} fusion(bf16[512,2048]{0,1:T(8,128)(2,1)S(1)} %get-tuple-element.254, s32[1024]{0:T(1024)S(1)} %fusion.90), kind=kCustom, calls=%fused_computation.2.clone.clone.1 | custom fusion | bytes 2101248 | tf_op jit(solution)/shard_map/while/body/eval_jaxpr/jit(_take)/gather | solution.py:16
  122.5 2.9 copy.14
  125.4 52.6 %while.20 = (s32[]{:T(128)}, f32[8,16,512]{2,1,0:T(8,128)S(1)}, s32[8,16,64]{2,1,0:T(8,128)S(1)}, bf16[512,2048]{0,1:T(8,128)(2,1)S(1)}, bf16[8,16,64]{2,1,0:T(8...) while((s32[]{:T(128)}, f32[8,16,512]{2,1,0:T(8,128)S(1)}, ...), condition=%wide.region_2.5_spmd, body=%wide.region_0.4_spmd.sunk | while | flops 70291552 | bytes 6755201 | solution.py:29
  126.2 4.0 %gather_fusion = bf16[1024,512]{1,0:T(8,128)(2,1)S(1)} fusion(bf16[512,2048]{0,1:T(8,128)(2,1)S(1)} %get-tuple-element.278, s32[1024]{0:T(1024)S(1)} %fusion.86), kind=kCustom, calls=%fused_computation.clone.clone.1 | custom fusion | bytes 2101248 | tf_op jit(solution)/shard_map/while/body/eval_jaxpr/jit(_take)/gather | solution.py:16
  132.8 4.0 %gather_fusion = bf16[1024,512]{1,0:T(8,128)(2,1)S(1)} fusion(bf16[512,2048]{0,1:T(8,128)(2,1)S(1)} %get-tuple-element.278, s32[1024]{0:T(1024)S(1)} %fusion.86), kind=kCustom, calls=%fused_computation.clone.clone.1 | custom fusion | bytes 2101248 | tf_op jit(solution)/shard_map/while/body/eval_jaxpr/jit(_take)/gather | solution.py:16
  139.3 4.0 %gather_fusion = bf16[1024,512]{1,0:T(8,128)(2,1)S(1)} fusion(bf16[512,2048]{0,1:T(8,128)(2,1)S(1)} %get-tuple-element.278, s32[1024]{0:T(1024)S(1)} %fusion.86), kind=kCustom, calls=%fused_computation.clone.clone.1 | custom fusion | bytes 2101248 | tf_op jit(solution)/shard_map/while/body/eval_jaxpr/jit(_take)/gather | solution.py:16
  145.9 4.0 %gather_fusion = bf16[1024,512]{1,0:T(8,128)(2,1)S(1)} fusion(bf16[512,2048]{0,1:T(8,128)(2,1)S(1)} %get-tuple-element.278, s32[1024]{0:T(1024)S(1)} %fusion.86), kind=kCustom, calls=%fused_computation.clone.clone.1 | custom fusion | bytes 2101248 | tf_op jit(solution)/shard_map/while/body/eval_jaxpr/jit(_take)/gather | solution.py:16
  152.5 4.0 %gather_fusion = bf16[1024,512]{1,0:T(8,128)(2,1)S(1)} fusion(bf16[512,2048]{0,1:T(8,128)(2,1)S(1)} %get-tuple-element.278, s32[1024]{0:T(1024)S(1)} %fusion.86), kind=kCustom, calls=%fused_computation.clone.clone.1 | custom fusion | bytes 2101248 | tf_op jit(solution)/shard_map/while/body/eval_jaxpr/jit(_take)/gather | solution.py:16
  159.0 4.0 %gather_fusion = bf16[1024,512]{1,0:T(8,128)(2,1)S(1)} fusion(bf16[512,2048]{0,1:T(8,128)(2,1)S(1)} %get-tuple-element.278, s32[1024]{0:T(1024)S(1)} %fusion.86), kind=kCustom, calls=%fused_computation.clone.clone.1 | custom fusion | bytes 2101248 | tf_op jit(solution)/shard_map/while/body/eval_jaxpr/jit(_take)/gather | solution.py:16
  163.2 1.5 fusion.87
  165.6 4.0 %gather_fusion = bf16[1024,512]{1,0:T(8,128)(2,1)S(1)} fusion(bf16[512,2048]{0,1:T(8,128)(2,1)S(1)} %get-tuple-element.278, s32[1024]{0:T(1024)S(1)} %fusion.86), kind=kCustom, calls=%fused_computation.clone.clone.1 | custom fusion | bytes 2101248 | tf_op jit(solution)/shard_map/while/body/eval_jaxpr/jit(_take)/gather | solution.py:16
  172.2 4.0 %gather_fusion = bf16[1024,512]{1,0:T(8,128)(2,1)S(1)} fusion(bf16[512,2048]{0,1:T(8,128)(2,1)S(1)} %get-tuple-element.278, s32[1024]{0:T(1024)S(1)} %fusion.86), kind=kCustom, calls=%fused_computation.clone.clone.1 | custom fusion | bytes 2101248 | tf_op jit(solution)/shard_map/while/body/eval_jaxpr/jit(_take)/gather | solution.py:16
  179.2 2.2 fusion.18
  183.9 113.8 %all-reduce.6.cloned.1.call-done = (f32[256,512]{1,0:T(8,128)}, f32[256,512]{1,0:T(8,128)}) async-done(((f32[256,512]{1,0:T(8,128)}, f32[256,512]{1,0:T(8,128)}), (f32[256,512]{1,0:T(8,128)}, f32[256,512]{1,0:T(8,128)})) %all-reduce.6.cloned.1.call-update) | async-done | bytes 1048592 | tf_op jit(solution)/shard_map/psum | solution.py:75
  299.8 30.7 %all-reduce.3 = (f32[17,17]{0,1:T(8,128)S(1)}, f32[17,8]{1,0:T(8,128)S(1)}, f32[17,17]{0,1:T(8,128)S(1)}, f32[17,8]{1,0:T(8,128)S(1)}) all-reduce(f32[17,17]{0,1:T(8,128)S(1)} %fusion.22, f32[17,8]{1,0:T(8,128)S(1)} %fusion.20, f32[17,17]{0,1:T(8,128)S(1)} %fusion.27, ...), channel_id=1, replica_groups=mesh['set'=32,'path'=8] {'path'}, use_global_device_ids=true, to_apply=%region_12.18 | all-reduce | flops 850 | bytes 6800 | tf_op jit(solution)/shard_map/psum | solution.py:79
  330.6 1.5 cholesky.55
  336.4 1.5 cholesky.44
  (230 shorter events, 53.0 us)
Async XLA Ops:
  7.2 5.4 %copy-start.4 = (f32[2048]{0:T(1024)S(1)}, f32[2048]{0:T(1024)}, u32[]{:S(2)}) copy-start(f32[2048]{0:T(1024)} %param.25) | copy-start | bytes 24580
  7.2 5.4 %copy-start.3 = (bf16[2,16,2048]{2,1,0:T(8,128)(2,1)S(1)}, bf16[2,16,2048]{2,1,0:T(8,128)(2,1)}, u32[]{:S(2)}) copy-start(bf16[2,16,2048]{2,1,0:T(8,128)(2,1)} %param.23) | copy-start | bytes 393220
  7.2 59.2 %all-gather.5.cloned.1.call-start = ((), (), s32[]{:S(2)}) async-start(), calls=%async_computation.1 | async-start | bytes 2162688 | tf_op jit(solution)/shard_map/all_gather | solution.py:66
  7.2 5.9 %copy-start = (bf16[2048,2048]{1,0:T(8,128)(2,1)S(1)}, bf16[2048,2048]{1,0:T(8,128)(2,1)}, u32[]{:S(2)}) copy-start(bf16[2048,2048]{1,0:T(8,128)(2,1)} %param.24) | copy-start | bytes 25165828
  13.1 2.7 copy-start.8
  13.1 2.8 copy-start.6
  13.1 2.9 copy-start.5
  13.1 3.0 copy-start.1
  15.0 106.8 %all-gather.3.cloned.1.call-start = ((), (), s32[]{:S(2)}) async-start(), calls=%async_computation | async-start | bytes 2162688 | tf_op jit(solution)/shard_map/all_gather | solution.py:66
  15.8 281.9 %all-reduce.6.cloned.1.call-start = ((), (), s32[]{:S(2)}) async-start(), calls=%async_computation.2 | async-start | bytes 2097152 | tf_op jit(solution)/shard_map/psum | solution.py:75
  121.8 0.7 copy-start.2
  125.4 52.6 %copy-start.7 = (s32[128]{0:T(128)S(1)}, s32[128]{0:T(128)}, u32[]{:S(2)}) copy-start(s32[128]{0:T(128)} %param.30) | copy-start | bytes 1540
Sparse Core Ops, SparseCore 0:
  15.2 51.1 all-gather.4
  68.9 47.9 all-gather.2
  181.5 116.0 all-reduce.5
where the time goes:
time: 350 us; the launch traced here: 349 us
  waiting for transfers between devices  160 us (46%)
  local copies, waits for them, and re-layouts  87.9 us (25%)
  matrix products  40.6 us (12%)
  blocking collectives  30.7 us (9%)
  other arithmetic  14.4 us (4%)
  between operations  14 us (4%)
    psum x1, waiting for transfers between devices, per_device(): summed = lax.psum(jnp.dot(onehot, values, precision=high), 'set')  114 us
    gather x16, local copies, waits for them, and re-layouts, value_block(): jnp.take(slab, lists_b.reshape(-1), axis=1)  63.4 us
    all_gather x2, waiting for transfers between devices, per_device(): piece = lax.all_gather(slab, 'set', axis=0, tiled=True)  45.7 us
    psum x1, blocking collectives, per_device(): lax.psum((jnp.dot(basis, basis.T, precision=high), jnp.dot(basis, netted....  30.7 us
    dot_general x16, matrix products, value_block(): jnp.einsum('psk,skl->psl', picked, gamma_b, preferred_element_type=jnp.fl...  24.4 us
    gather x16, local copies, waits for them, and re-layouts, value_block(): rates = jnp.exp(0.2 * jnp.take(slab, cur_b, axis=1).astype(jnp.float32))  9.44 us
    dot_general x2, matrix products, per_device(): jnp.dot(shocks[step], loading, preferred_element_type=jnp.float32)  7.25 us
  transfers between devices with their start and end apart: 3, of which 2 were waited for; matrix products, arithmetic and copies ran while one was open for 18% of the time, Pallas kernels for 0%

commit v1 on v0

--- a/solution.py
+++ b/solution.py
@@ -72,7 +72,7 @@
     for step in range(STEPS):
         values = evaluated[step][:set_count]
         factors = evaluated[step][set_count:]
-        summed = lax.psum(jnp.dot(onehot, values, precision=high), "set")
+        summed = jnp.sum(lax.all_gather(jnp.dot(onehot, values, precision=high), "set"), axis=0)
         netted = lax.dynamic_slice_in_dim(summed, member * CP_DEV, CP_DEV, 0)
         ones = jnp.ones((1, values.shape[1]), jnp.float32)
         basis = jnp.concatenate([ones, factors], axis=0)

time: 350 us -> 334 us (0.954)
  waiting for transfers between devices: 160 us -> 130 us
  other arithmetic: 14.4 us -> 29.9 us
    psum x1 -> x0, waiting for transfers between devices: 114 us -> none  [per_device(): summed = lax.psum(jnp.dot(onehot, values, precision=high), 'set')]
    all_gather x0 -> x2, waiting for transfers between devices: none -> 89.4 us  [per_device(): lax.all_gather(jnp.dot(onehot, values, precision=high), 'set')]
    reduce_sum x0 -> x2, other arithmetic: none -> 15.5 us  [per_device(): jnp.sum(lax.all_gather(jnp.dot(onehot, values, precision=high), 'set'), a...]
    all_gather x2, waiting for transfers between devices: 45.7 us -> 40.9 us  [per_device(): piece = lax.all_gather(slab, 'set', axis=0, tiled=True)]
  transfers between devices with their start and end apart: 3 -> 4, of which waited for: 2 -> 3; matrix products, arithmetic and copies ran while one was open for 18% -> 40% of each run, Pallas kernels for 0% -> 0%
where the time goes in v1:
time: 334 us
  waiting for transfers between devices  130 us (39%)
  local copies, waits for them, and re-layouts  86.8 us (26%)
  matrix products  40.1 us (12%)
  blocking collectives  30.7 us (9%)
  other arithmetic  29.9 us (9%)
  between operations  14 us (4%)
    all_gather x2, waiting for transfers between devices, per_device(): lax.all_gather(jnp.dot(onehot, values, precision=high), 'set')  89.4 us
    gather x16, local copies, waits for them, and re-layouts, value_block(): jnp.take(slab, lists_b.reshape(-1), axis=1)  63.4 us
    all_gather x2, waiting for transfers between devices, per_device(): piece = lax.all_gather(slab, 'set', axis=0, tiled=True)  40.9 us
    psum x1, blocking collectives, per_device(): lax.psum((jnp.dot(basis, basis.T, precision=high), jnp.dot(basis, netted....  30.7 us
    dot_general x16, matrix products, value_block(): jnp.einsum('psk,skl->psl', picked, gamma_b, preferred_element_type=jnp.fl...  24.4 us
    reduce_sum x2, other arithmetic, per_device(): jnp.sum(lax.all_gather(jnp.dot(onehot, values, precision=high), 'set'), a...  15.5 us
    dot_general x2, matrix products, per_device(): jnp.dot(shocks[step], loading, preferred_element_type=jnp.float32)  10.6 us
    gather x16, local copies, waits for them, and re-layouts, value_block(): rates = jnp.exp(0.2 * jnp.take(slab, cur_b, axis=1).astype(jnp.float32))  9.44 us
  transfers between devices with their start and end apart: 4, of which 3 were waited for; matrix products, arithmetic and copies ran while one was open for 40% of the time, Pallas kernels for 0%

profile of v1, /device:TPU:6, one launch (start us, length us, event | category | flops | bytes accessed | tf_op | source)
XLA Modules:
  0.0 333.5 jit_solution(13971584882055103625)
XLA Ops:
  7.2 5.2 %fusion.65 = (bf16[16,2048]{1,0:T(8,128)(2,1)}, f32[16,2048]{1,0:T(8,128)S(1)}) fusion(bf16[2048,2048]{1,0:T(8,128)(2,1)} %param.24, bf16[2,16,2048]{2,1,0:T(8,128)(2,1)} %param.23, f32[16,2048]{1,0:T(8,128)} %param.22, f32[2048]{0:T(1024)} %param.25), kind=kOutput, calls=%fused_computation.112 | convolution fusion | flops 134316032 | bytes 8790016 | tf_op jit(solution)/shard_map/dot_general | solution.py:61
  12.6 5.3 %fusion.64 = (bf16[16,2048]{1,0:T(8,128)(2,1)}, f32[16,2048]{1,0:T(8,128)}) fusion(bf16[2048,2048]{1,0:T(8,128)(2,1)} %param.24, bf16[2,16,2048]{2,1,0:T(8,128)(2,1)S(1)} %copy-done.1, f32[16,2048]{1,0:T(8,128)S(1)} %get-tuple-element.136, f32[2048]{0:T(1024)S(1)} %copy-done.2), kind=kOutput, calls=%fused_computation.111 | convolution fusion | flops 134316032 | bytes 8790016 | tf_op jit(solution)/shard_map/dot_general | solution.py:61
  18.4 4.5 %copy.13 = bf16[128,64,64]{1,2,0:T(8,128)(2,1)} copy(bf16[128,64,64]{0,2,1:T(8,128)(2,1)S(1)} %copy-done) | data formatting | bytes 2097152 | tf_op args[6]
  22.9 40.9 %all-gather.7.cloned.1.call-done = bf16[512,2048]{1,0:T(8,128)(2,1)} async-done(((bf16[16,2048]{1,0:T(8,128)(2,1)}), bf16[512,2048]{1,0:T(8,128)(2,1)}) %all-gather.7.cloned.1.call-update) | async-done | bytes 2097168 | tf_op jit(solution)/shard_map/all_gather | solution.py:66
  63.8 2.9 copy.14
  66.7 52.6 %while.20 = (s32[]{:T(128)}, f32[8,16,512]{2,1,0:T(8,128)S(1)}, s32[8,16,64]{2,1,0:T(8,128)S(1)}, bf16[512,2048]{0,1:T(8,128)(2,1)S(1)}, bf16[8,16,64]{2,1,0:T(8...) while((s32[]{:T(128)}, f32[8,16,512]{2,1,0:T(8,128)S(1)}, ...), condition=%wide.region_2.5_spmd, body=%wide.region_0.4_spmd.sunk | while | flops 70291552 | bytes 6755201 | solution.py:29
  67.5 4.0 %gather_fusion = bf16[1024,512]{1,0:T(8,128)(2,1)S(1)} fusion(bf16[512,2048]{0,1:T(8,128)(2,1)S(1)} %get-tuple-element.276, s32[1024]{0:T(1024)S(1)} %fusion.86), kind=kCustom, calls=%fused_computation.clone.clone.1 | custom fusion | bytes 2101248 | tf_op jit(solution)/shard_map/while/body/eval_jaxpr/jit(_take)/gather | solution.py:16
  74.0 4.0 %gather_fusion = bf16[1024,512]{1,0:T(8,128)(2,1)S(1)} fusion(bf16[512,2048]{0,1:T(8,128)(2,1)S(1)} %get-tuple-element.276, s32[1024]{0:T(1024)S(1)} %fusion.86), kind=kCustom, calls=%fused_computation.clone.clone.1 | custom fusion | bytes 2101248 | tf_op jit(solution)/shard_map/while/body/eval_jaxpr/jit(_take)/gather | solution.py:16
  80.6 4.0 %gather_fusion = bf16[1024,512]{1,0:T(8,128)(2,1)S(1)} fusion(bf16[512,2048]{0,1:T(8,128)(2,1)S(1)} %get-tuple-element.276, s32[1024]{0:T(1024)S(1)} %fusion.86), kind=kCustom, calls=%fused_computation.clone.clone.1 | custom fusion | bytes 2101248 | tf_op jit(solution)/shard_map/while/body/eval_jaxpr/jit(_take)/gather | solution.py:16
  87.2 4.0 %gather_fusion = bf16[1024,512]{1,0:T(8,128)(2,1)S(1)} fusion(bf16[512,2048]{0,1:T(8,128)(2,1)S(1)} %get-tuple-element.276, s32[1024]{0:T(1024)S(1)} %fusion.86), kind=kCustom, calls=%fused_computation.clone.clone.1 | custom fusion | bytes 2101248 | tf_op jit(solution)/shard_map/while/body/eval_jaxpr/jit(_take)/gather | solution.py:16
  93.7 4.0 %gather_fusion = bf16[1024,512]{1,0:T(8,128)(2,1)S(1)} fusion(bf16[512,2048]{0,1:T(8,128)(2,1)S(1)} %get-tuple-element.276, s32[1024]{0:T(1024)S(1)} %fusion.86), kind=kCustom, calls=%fused_computation.clone.clone.1 | custom fusion | bytes 2101248 | tf_op jit(solution)/shard_map/while/body/eval_jaxpr/jit(_take)/gather | solution.py:16
  100.3 4.0 %gather_fusion = bf16[1024,512]{1,0:T(8,128)(2,1)S(1)} fusion(bf16[512,2048]{0,1:T(8,128)(2,1)S(1)} %get-tuple-element.276, s32[1024]{0:T(1024)S(1)} %fusion.86), kind=kCustom, calls=%fused_computation.clone.clone.1 | custom fusion | bytes 2101248 | tf_op jit(solution)/shard_map/while/body/eval_jaxpr/jit(_take)/gather | solution.py:16
  106.9 4.0 %gather_fusion = bf16[1024,512]{1,0:T(8,128)(2,1)S(1)} fusion(bf16[512,2048]{0,1:T(8,128)(2,1)S(1)} %get-tuple-element.276, s32[1024]{0:T(1024)S(1)} %fusion.86), kind=kCustom, calls=%fused_computation.clone.clone.1 | custom fusion | bytes 2101248 | tf_op jit(solution)/shard_map/while/body/eval_jaxpr/jit(_take)/gather | solution.py:16
  113.5 4.0 %gather_fusion = bf16[1024,512]{1,0:T(8,128)(2,1)S(1)} fusion(bf16[512,2048]{0,1:T(8,128)(2,1)S(1)} %get-tuple-element.276, s32[1024]{0:T(1024)S(1)} %fusion.86), kind=kCustom, calls=%fused_computation.clone.clone.1 | custom fusion | bytes 2101248 | tf_op jit(solution)/shard_map/while/body/eval_jaxpr/jit(_take)/gather | solution.py:16
  120.8 2.9 copy.17
  123.7 52.6 %while.21 = (s32[]{:T(128)}, f32[8,16,512]{2,1,0:T(8,128)S(1)}, s32[8,16,64]{2,1,0:T(8,128)S(1)}, bf16[512,2048]{0,1:T(8,128)(2,1)S(1)}, bf16[8,16,64]{2,1,0:T(8...) while((s32[]{:T(128)}, f32[8,16,512]{2,1,0:T(8,128)S(1)}, ...), condition=%wide.region_10.16_spmd, body=%wide.region_8.15_spmd.sunk | while | flops 70291552 | bytes 6755201 | solution.py:29
  124.5 4.0 %gather_fusion.2 = bf16[1024,512]{1,0:T(8,128)(2,1)S(1)} fusion(bf16[512,2048]{0,1:T(8,128)(2,1)S(1)} %get-tuple-element.252, s32[1024]{0:T(1024)S(1)} %fusion.90), kind=kCustom, calls=%fused_computation.2.clone.clone.1 | custom fusion | bytes 2101248 | tf_op jit(solution)/shard_map/while/body/eval_jaxpr/jit(_take)/gather | solution.py:16
  131.0 4.0 %gather_fusion.2 = bf16[1024,512]{1,0:T(8,128)(2,1)S(1)} fusion(bf16[512,2048]{0,1:T(8,128)(2,1)S(1)} %get-tuple-element.252, s32[1024]{0:T(1024)S(1)} %fusion.90), kind=kCustom, calls=%fused_computation.2.clone.clone.1 | custom fusion | bytes 2101248 | tf_op jit(solution)/shard_map/while/body/eval_jaxpr/jit(_take)/gather | solution.py:16
  137.6 4.0 %gather_fusion.2 = bf16[1024,512]{1,0:T(8,128)(2,1)S(1)} fusion(bf16[512,2048]{0,1:T(8,128)(2,1)S(1)} %get-tuple-element.252, s32[1024]{0:T(1024)S(1)} %fusion.90), kind=kCustom, calls=%fused_computation.2.clone.clone.1 | custom fusion | bytes 2101248 | tf_op jit(solution)/shard_map/while/body/eval_jaxpr/jit(_take)/gather | solution.py:16
  144.2 4.0 %gather_fusion.2 = bf16[1024,512]{1,0:T(8,128)(2,1)S(1)} fusion(bf16[512,2048]{0,1:T(8,128)(2,1)S(1)} %get-tuple-element.252, s32[1024]{0:T(1024)S(1)} %fusion.90), kind=kCustom, calls=%fused_computation.2.clone.clone.1 | custom fusion | bytes 2101248 | tf_op jit(solution)/shard_map/while/body/eval_jaxpr/jit(_take)/gather | solution.py:16
  150.8 4.0 %gather_fusion.2 = bf16[1024,512]{1,0:T(8,128)(2,1)S(1)} fusion(bf16[512,2048]{0,1:T(8,128)(2,1)S(1)} %get-tuple-element.252, s32[1024]{0:T(1024)S(1)} %fusion.90), kind=kCustom, calls=%fused_computation.2.clone.clone.1 | custom fusion | bytes 2101248 | tf_op jit(solution)/shard_map/while/body/eval_jaxpr/jit(_take)/gather | solution.py:16
  157.3 4.0 %gather_fusion.2 = bf16[1024,512]{1,0:T(8,128)(2,1)S(1)} fusion(bf16[512,2048]{0,1:T(8,128)(2,1)S(1)} %get-tuple-element.252, s32[1024]{0:T(1024)S(1)} %fusion.90), kind=kCustom, calls=%fused_computation.2.clone.clone.1 | custom fusion | bytes 2101248 | tf_op jit(solution)/shard_map/while/body/eval_jaxpr/jit(_take)/gather | solution.py:16
  163.9 4.0 %gather_fusion.2 = bf16[1024,512]{1,0:T(8,128)(2,1)S(1)} fusion(bf16[512,2048]{0,1:T(8,128)(2,1)S(1)} %get-tuple-element.252, s32[1024]{0:T(1024)S(1)} %fusion.90), kind=kCustom, calls=%fused_computation.2.clone.clone.1 | custom fusion | bytes 2101248 | tf_op jit(solution)/shard_map/while/body/eval_jaxpr/jit(_take)/gather | solution.py:16
  170.5 4.0 %gather_fusion.2 = bf16[1024,512]{1,0:T(8,128)(2,1)S(1)} fusion(bf16[512,2048]{0,1:T(8,128)(2,1)S(1)} %get-tuple-element.252, s32[1024]{0:T(1024)S(1)} %fusion.90), kind=kCustom, calls=%fused_computation.2.clone.clone.1 | custom fusion | bytes 2101248 | tf_op jit(solution)/shard_map/while/body/eval_jaxpr/jit(_take)/gather | solution.py:16
  174.7 1.5 fusion.91
  180.0 18.0 %all-gather.11.cloned.1.call-done = f32[8192,512]{1,0:T(8,128)} async-done(((f32[256,512]{1,0:T(8,128)}), f32[8192,512]{1,0:T(8,128)}) %all-gather.11.cloned.1.call-update) | async-done | bytes 16777232 | tf_op jit(solution)/shard_map/all_gather | solution.py:75
  198.0 7.8 %reduce_sum.36 = f32[256,512]{1,0:T(8,128)S(1)} reduce(f32[32,256,512]{2,1,0:T(8,128)} %bitcast.139, f32[]{:T(128)} %constant.111.clone.1), dimensions={0}, to_apply=%region_3.6 | reduce | flops 4063232 | bytes 17301508 | tf_op jit(solution)/shard_map/reduce_sum | solution.py:75
  206.1 71.5 %all-gather.13.cloned.1.call-done = f32[8192,512]{1,0:T(8,128)} async-done(((f32[256,512]{1,0:T(8,128)}), f32[8192,512]{1,0:T(8,128)}) %all-gather.13.cloned.1.call-update) | async-done | bytes 16777232 | tf_op jit(solution)/shard_map/all_gather | solution.py:75
  277.5 7.8 %reduce_sum.37 = f32[256,512]{1,0:T(8,128)S(1)} reduce(f32[32,256,512]{2,1,0:T(8,128)} %bitcast.140, f32[]{:T(128)} %constant.111.clone.1), dimensions={0}, to_apply=%region_11.17 | reduce | flops 4063232 | bytes 17301508 | tf_op jit(solution)/shard_map/reduce_sum | solution.py:75
  285.6 30.7 %all-reduce.2 = (f32[17,17]{0,1:T(8,128)S(1)}, f32[17,8]{1,0:T(8,128)S(1)}, f32[17,17]{0,1:T(8,128)S(1)}, f32[17,8]{1,0:T(8,128)S(1)}) all-reduce(f32[17,17]{0,1:T(8,128)S(1)} %fusion.22, f32[17,8]{1,0:T(8,128)S(1)} %fusion.20, f32[17,17]{0,1:T(8,128)S(1)} %fusion.27, ...), channel_id=1, replica_groups=mesh['set'=32,'path'=8] {'path'}, use_global_device_ids=true, to_apply=%region_12.18 | all-reduce | flops 850 | bytes 6800 | tf_op jit(solution)/shard_map/psum | solution.py:79
  316.5 1.5 cholesky.55
  321.5 1.5 cholesky.44
  (231 shorter events, 52.8 us)
Async XLA Ops:
  7.2 5.4 %copy-start.2 = (f32[2048]{0:T(1024)S(1)}, f32[2048]{0:T(1024)}, u32[]{:S(2)}) copy-start(f32[2048]{0:T(1024)} %param.25) | copy-start | bytes 24580
  7.2 5.4 %copy-start.1 = (bf16[2,16,2048]{2,1,0:T(8,128)(2,1)S(1)}, bf16[2,16,2048]{2,1,0:T(8,128)(2,1)}, u32[]{:S(2)}) copy-start(bf16[2,16,2048]{2,1,0:T(8,128)(2,1)} %param.23) | copy-start | bytes 393220
  7.2 56.6 %all-gather.7.cloned.1.call-start = ((), (), s32[]{:S(2)}) async-start(), calls=%async_computation | async-start | bytes 2162688 | tf_op jit(solution)/shard_map/all_gather | solution.py:66
  12.5 108.3 %all-gather.9.cloned.1.call-start = ((), (), s32[]{:S(2)}) async-start(), calls=%async_computation.1 | async-start | bytes 2162688 | tf_op jit(solution)/shard_map/all_gather | solution.py:66
  12.6 5.5 %copy-start.6 = (s32[128]{0:T(128)S(1)}, s32[128]{0:T(128)}, u32[]{:S(2)}) copy-start(s32[128]{0:T(128)} %param.29) | copy-start | bytes 1540
  12.6 5.5 %copy-start.4 = (bf16[128,64]{0,1:T(8,128)(2,1)S(1)}, bf16[128,64]{0,1:T(8,128)(2,1)}, u32[]{:S(2)}) copy-start(bf16[128,64]{0,1:T(8,128)(2,1)} %param.27) | copy-start | bytes 49156
  12.6 5.7 %copy-start.3 = (s32[128,64]{0,1:T(8,128)S(1)}, s32[128,64]{0,1:T(8,128)}, u32[]{:S(2)}) copy-start(s32[128,64]{0,1:T(8,128)} %param.26) | copy-start | bytes 98308
  12.6 5.7 %copy-start = (bf16[128,64,64]{0,2,1:T(8,128)(2,1)S(1)}, bf16[128,64,64]{0,2,1:T(8,128)(2,1)}, u32[]{:S(2)}) copy-start(bf16[128,64,64]{0,2,1:T(8,128)(2,1)} %param.28) | copy-start | bytes 3145732
  18.0 180.0 %all-gather.11.cloned.1.call-start = ((), (), s32[]{:S(2)}) async-start(), calls=%async_computation.2 | async-start | bytes 17301504 | tf_op jit(solution)/shard_map/all_gather | solution.py:75
  66.7 52.6 %copy-start.5 = (s32[128]{0:T(128)S(1)}, s32[128]{0:T(128)}, u32[]{:S(2)}) copy-start(s32[128]{0:T(128)} %param.30) | copy-start | bytes 1540
  120.5 157.0 %all-gather.13.cloned.1.call-start = ((), (), s32[]{:S(2)}) async-start(), calls=%async_computation.3 | async-start | bytes 17301504 | tf_op jit(solution)/shard_map/all_gather | solution.py:75
Sparse Core Ops, SparseCore 0:
  12.6 51.1 all-gather.6
  66.3 47.9 all-gather.8
  120.7 77.2 all-gather.10
  200.4 77.0 all-gather.12
